TPU v7x, 256 devices: a whole 4x4x8 slice. The times are simulated.
256 devices in a mesh: row: 16 (over z, core), col: 16 (over y, x).
Axes of the slice: x: 4, y: 4, z: 8, core: 2. Of those that a mesh axis runs over, the one named last changes fastest.
Arguments:
- start_block: float32 [4096, 64, 128], P(('row', 'col')), may hold values from -2700 to 2700
- tile_values: bfloat16 [65536, 128, 128], P(('row', 'col')), may hold values from -3.535534 to 3.535534
- tile_rows: int32 [65536], P(('row', 'col')), may hold values from 0 to 15
- tile_cols: int32 [65536], P(('row', 'col')), may hold values from 0 to 79
- tile_count: int32 [256], P(('row', 'col')), may hold values from 32 to 256, as said below
- send_rows: int32 [256, 256, 32], P(('row', 'col')), may hold values from 0 to 2047
- send_count: int32 [256, 256], P(('row', 'col')), may hold values from 16 to 32, as said below
- rotation: float32 [192, 64], replicated, may hold values from -0.4375 to 0.4375
Outputs:
- embedding: float32 [4096, 64, 128], P(('row', 'col'))
Inputs may be any that keep to these rules, and one draw needn't show every extreme that they name: `tile_cols`: source tiles below 16 are the partition's own row tiles, the others its halo tiles. `tile_count`: slots at or past the count are ignored; some partition fills all 256 slots. `send_count`: slots at or past the count carry zeros; every partition fills all 32 slots for some peer, and some partition receives 32 rows from every partition.
All inputs are finite; a program needn't handle non-finite values.
Results may differ from a plain program's by a relative error of at most 0.0029.
Values may be sent and summed in bfloat16 or wider, within the bound.
A program may use at most 64 MiB of HBM per device.

v0:
```python
import jax
import jax.numpy as jnp
from jax import lax
from jax.sharding import PartitionSpec as P

HIGHEST_PRECISION = lax.Precision.HIGHEST


def local_inner(left_block, right_block):
    return jnp.einsum("tai,tbi->ab", left_block, right_block, precision=HIGHEST_PRECISION)


def unit_columns(product_block, gram_matrix):
    factor = jnp.linalg.cholesky(gram_matrix)
    inverse = lax.linalg.triangular_solve(
        factor, jnp.eye(factor.shape[0], dtype=jnp.float32), left_side=True, lower=True
    )
    return jnp.einsum("ab,tbi->tai", inverse, product_block, precision=HIGHEST_PRECISION)


def apply_graph(current, tile_values, tile_rows, tile_cols, tile_count, send_rows, send_count):
    row_tiles, block_width, tile_size = current.shape
    rounded = current.astype(jnp.bfloat16)
    node_rows = rounded.transpose(0, 2, 1).reshape(row_tiles * tile_size, block_width)
    targets = send_rows[0]
    partitions, capacity = targets.shape
    chosen = node_rows[targets.reshape(-1)].reshape(partitions, capacity, block_width)
    kept_slots = jnp.arange(capacity, dtype=jnp.int32)[None, :] < send_count[0][:, None]
    chosen = jnp.where(kept_slots[:, :, None], chosen, jnp.zeros_like(chosen))
    outgoing = chosen.reshape(lax.axis_size("row"), lax.axis_size("col"), capacity * block_width)
    incoming = lax.all_to_all(
        lax.all_to_all(outgoing, "row", split_axis=0, concat_axis=0, tiled=True),
        "col",
        split_axis=1,
        concat_axis=1,
        tiled=True,
    )
    halo_count = partitions * capacity // tile_size
    halo_block = incoming.reshape(halo_count, tile_size, block_width).transpose(0, 2, 1)
    source = jnp.concatenate([rounded, halo_block], 0)
    picked = source[tile_cols]
    products = jnp.einsum("kbj,kij->kbi", picked, tile_values, preferred_element_type=jnp.float32)
    slot_total = tile_cols.shape[0]
    live_slots = jnp.arange(slot_total, dtype=jnp.int32) < tile_count[0]
    owner_table = (
        tile_rows[None, :] == jnp.arange(row_tiles, dtype=jnp.int32)[:, None]
    ) & live_slots[None, :]
    return jnp.einsum(
        "rk,kbi->rbi", owner_table.astype(jnp.float32), products, precision=HIGHEST_PRECISION
    )


def body(
    start_block, tile_values, tile_rows, tile_cols, tile_count, send_rows, send_count, rotation
):
    node_total = (
        start_block.shape[0] * start_block.shape[2] * lax.axis_size("row") * lax.axis_size("col")
    )
    start_sum = lax.psum(local_inner(start_block, start_block), ("row", "col"))
    vectors = [unit_columns(start_block, start_sum / node_total)]
    for krylov_step in range(2):
        product_block = apply_graph(
            vectors[-1], tile_values, tile_rows, tile_cols, tile_count, send_rows, send_count
        )
        stacked = jnp.concatenate(vectors, 1)
        coefficients = lax.psum(local_inner(stacked, product_block), ("row", "col")) / node_total
        residual_block = product_block - jnp.einsum(
            "ab,tai->tbi", coefficients, stacked, precision=HIGHEST_PRECISION
        )
        gram_matrix = (
            lax.psum(local_inner(residual_block, residual_block), ("row", "col")) / node_total
        )
        vectors.append(unit_columns(residual_block, gram_matrix))
    all_vectors = jnp.concatenate(vectors, 1)
    return jnp.einsum("jb,tji->tbi", rotation, all_vectors, precision=HIGHEST_PRECISION)


def solution(mesh):
    return jax.shard_map(
        body,
        mesh=mesh,
        in_specs=(
            P(("row", "col"), None, None),
            P(("row", "col"), None, None),
            P(("row", "col")),
            P(("row", "col")),
            P(("row", "col")),
            P(("row", "col"), None, None),
            P(("row", "col"), None),
            P(),
        ),
        out_specs=P(("row", "col"), None, None),
        check_vma=False,
    )
```

profile of v0, /device:TPU:1, one launch (start us, length us, event | category | flops | bytes accessed | tf_op | source)
XLA Modules:
  0.0 668.5 jit_solution(7324829424072807957)
XLA Ops:
  1.6 81.5 %psum.35 = f32[64,64]{0,1:T(8,128)S(1)} all-reduce(f32[64,64]{0,1:T(8,128)S(1)} %convolution_bitcast_fusion.8), channel_id=1, replica_groups=mesh['row'=16,'col'=16] {'row','col'}, use_global_device_ids=true, to_apply=%region_0.0 | all-reduce | flops 4096 | bytes 32768 | tf_op jit(solution)/shard_map/psum | solution.py:59
  83.2 5.8 cholesky.59
  90.4 4.9 custom-call.7
  96.8 24.0 %gather_fusion = bf16[8192,64]{1,0:T(8,128)(2,1)S(1)} fusion(bf16[2048,64]{1,0:T(8,128)(2,1)S(1)} %bitcast.92, s32[8192]{0:T(1024)S(1)} %broadcast_clamp_fusion), kind=kCustom, calls=%fused_computation | custom fusion | bytes 2129920 | tf_op jit(solution)/shard_map/gather | solution.py:27
  120.9 2.4 reshape.93
  123.4 2.1 broadcast_in_dim.16
  128.8 33.5 %all_to_all.20 = bf16[16,16,2048]{2,1,0:T(8,128)(2,1)S(1)} all-to-all(bf16[16,16,2048]{2,1,0:T(8,128)(2,1)S(1)} %broadcast_select_fusion.1), channel_id=1, replica_groups=mesh['row'=16,'col'=16] {'row'}, dimensions={0} | all-to-all | bytes 2097152 | tf_op jit(solution)/shard_map/all_to_all | solution.py:32
  163.9 3.9 all-to-all-start.1
  168.7 16.5 %all-to-all-done.1 = bf16[16,16,2048]{2,0,1:T(8,128)(2,1)S(1)} async-done(((bf16[16,16,2048]{2,0,1:T(8,128)(2,1)}), bf16[16,16,2048]{2,0,1:T(8,128)(2,1)S(1)}, u32[]{:S(2)}, u32[]{:S(2)}) %all-to-all-start.1) | async-done | bytes 1048608 | tf_op jit(solution)/shard_map/all_to_all | solution.py:31
  186.8 3.3 reshape.94
  190.2 2.1 pad_maximum_fusion
  192.2 10.4 %gather_fusion.1 = bf16[256,64,128]{1,2,0:T(8,128)(2,1)} fusion(bf16[80,64,128]{1,2,0:T(8,128)(2,1)} %pad_maximum_fusion, s32[1024]{0:T(1024)S(1)} %pad_clamp_fusion), kind=kCustom, calls=%fused_computation.1 | custom fusion | bytes 8389632 | tf_op jit(solution)/shard_map/gather | solution.py:41
  202.6 9.7 %fusion.57 = f32[256,64,128]{2,1,0:T(8,128)S(1)} fusion(bf16[256,64,128]{1,2,0:T(8,128)(2,1)} %gather_fusion.1, bf16[256,128,128]{2,1,0:T(8,128)(2,1)} %param.12), kind=kOutput, calls=%fused_computation.100 | convolution fusion | flops 536870912 | bytes 20971520 | tf_op jit(solution)/shard_map/kbj,kij->kbi/dot_general | solution.py:42
  212.3 7.5 %fusion.2 = f32[16,64,128]{2,0,1:T(8,128)S(1)} fusion(f32[256,64,128]{2,1,0:T(8,128)S(1)} %fusion.57, s32[256]{0:T(256)S(1)} %copy-done.6, pred[256]{0:T(512)(128)(4,1)S(1)} %iota_compare_fusion.7), kind=kOutput, calls=%fused_computation.6 | convolution fusion | flops 402661376 | bytes 8914176 | tf_op jit(solution)/shard_map/rk,kbi->rbi/dot_general | solution.py:48
  220.5 72.7 %psum.36 = f32[64,64]{0,1:T(8,128)S(1)} all-reduce(f32[64,64]{0,1:T(8,128)S(1)} %convolution_bitcast_fusion.6), channel_id=1, replica_groups=mesh['row'=16,'col'=16] {'row','col'}, use_global_device_ids=true, to_apply=%region_3.0 | all-reduce | flops 4096 | bytes 32768 | tf_op jit(solution)/shard_map/psum | solution.py:66
  295.0 73.9 %psum.37 = f32[64,64]{0,1:T(8,128)S(1)} all-reduce(f32[64,64]{0,1:T(8,128)S(1)} %convolution_bitcast_fusion.5), channel_id=1, replica_groups=mesh['row'=16,'col'=16] {'row','col'}, use_global_device_ids=true, to_apply=%region_4.0 | all-reduce | flops 4096 | bytes 32768 | tf_op jit(solution)/shard_map/psum | solution.py:71
  369.0 5.8 cholesky.70
  376.3 4.9 custom-call.8
  383.3 24.0 %gather_fusion.2 = bf16[8192,64]{1,0:T(8,128)(2,1)S(1)} fusion(bf16[2048,64]{1,0:T(8,128)(2,1)S(1)} %bitcast.93, s32[8192]{0:T(1024)S(1)} %broadcast_clamp_fusion), kind=kCustom, calls=%fused_computation.2 | custom fusion | bytes 2129920 | tf_op jit(solution)/shard_map/gather | solution.py:27
  407.4 2.4 reshape.96
  411.3 32.6 %all_to_all.21 = bf16[16,16,2048]{2,1,0:T(8,128)(2,1)S(1)} all-to-all(bf16[16,16,2048]{2,1,0:T(8,128)(2,1)S(1)} %broadcast_select_fusion), channel_id=1, replica_groups=mesh['row'=16,'col'=16] {'row'}, dimensions={0} | all-to-all | bytes 2097152 | tf_op jit(solution)/shard_map/all_to_all | solution.py:32
  445.5 3.9 all-to-all-start.3
  449.7 18.4 %all-to-all-done.3 = bf16[16,16,2048]{2,0,1:T(8,128)(2,1)S(1)} async-done(((bf16[16,16,2048]{2,0,1:T(8,128)(2,1)}), bf16[16,16,2048]{2,0,1:T(8,128)(2,1)S(1)}, u32[]{:S(2)}, u32[]{:S(2)}) %all-to-all-start.3) | async-done | bytes 1048608 | tf_op jit(solution)/shard_map/all_to_all | solution.py:31
  469.7 3.3 reshape.97
  473.0 2.1 pad_maximum_fusion.1
  475.1 10.4 %gather_fusion.3 = bf16[256,64,128]{1,2,0:T(8,128)(2,1)} fusion(bf16[80,64,128]{1,2,0:T(8,128)(2,1)} %pad_maximum_fusion.1, s32[1024]{0:T(1024)S(1)} %pad_clamp_fusion), kind=kCustom, calls=%fused_computation.3 | custom fusion | bytes 8389632 | tf_op jit(solution)/shard_map/gather | solution.py:41
  485.5 9.5 %fusion.58 = f32[256,64,128]{2,1,0:T(8,128)S(1)} fusion(bf16[256,64,128]{1,2,0:T(8,128)(2,1)} %gather_fusion.3, bf16[256,128,128]{2,1,0:T(8,128)(2,1)} %param.12), kind=kOutput, calls=%fused_computation.101 | convolution fusion | flops 536870912 | bytes 20971520 | tf_op jit(solution)/shard_map/kbj,kij->kbi/dot_general | solution.py:42
  495.0 7.5 %fusion = f32[16,64,128]{2,0,1:T(8,128)S(1)} fusion(f32[256,64,128]{2,1,0:T(8,128)S(1)} %fusion.58, s32[256]{0:T(256)S(1)} %copy-done.6, pred[256]{0:T(512)(128)(4,1)S(1)} %iota_compare_fusion.7), kind=kOutput, calls=%fused_computation.4 | convolution fusion | flops 402661376 | bytes 8914176 | tf_op jit(solution)/shard_map/rk,kbi->rbi/dot_general | solution.py:48
  503.7 72.8 %psum.38 = f32[128,64]{0,1:T(8,128)S(1)} all-reduce(f32[128,64]{0,1:T(8,128)S(1)} %convolution_bitcast_fusion.1), channel_id=1, replica_groups=mesh['row'=16,'col'=16] {'row','col'}, use_global_device_ids=true, to_apply=%region_5.8 | all-reduce | flops 8192 | bytes 65536 | tf_op jit(solution)/shard_map/psum | solution.py:66
  578.3 74.5 %psum.39 = f32[64,64]{0,1:T(8,128)S(1)} all-reduce(f32[64,64]{0,1:T(8,128)S(1)} %convolution_bitcast_fusion.3), channel_id=1, replica_groups=mesh['row'=16,'col'=16] {'row','col'}, use_global_device_ids=true, to_apply=%region_6.9 | all-reduce | flops 4096 | bytes 32768 | tf_op jit(solution)/shard_map/psum | solution.py:71
  652.9 5.8 cholesky.81
  660.1 4.9 custom-call.9
  (72 shorter events, 29.6 us)
Async XLA Ops:
  0.0 1.0 copy-start
  0.0 96.5 %copy-start.5 = (s32[1,256,32]{1,2,0:T(8,128)S(1)}, s32[1,256,32]{1,2,0:T(8,128)}, u32[]{:S(2)}) copy-start(s32[1,256,32]{1,2,0:T(8,128)} %param.16) | copy-start | bytes 98308
  96.8 26.5 %copy-start.7 = (s32[1,256]{1,0:T(1,128)S(1)}, s32[1,256]{1,0:T(1,128)}, u32[]{:S(2)}) copy-start(s32[1,256]{1,0:T(1,128)} %param.17) | copy-start | bytes 3076
  127.3 36.6 %copy-start.3 = (pred[16,16,2048]{2,1,0:T(8,128)(4,1)}, pred[16,16,2048]{2,1,0:T(8,128)(4,1)S(1)}, u32[]{:S(2)}) copy-start(pred[16,16,2048]{2,1,0:T(8,128)(4,1)S(1)} %broadcast_in_dim.17) | copy-start | bytes 1572868
  128.8 39.9 %copy-start.8 = (s32[256]{0:T(256)S(1)}, s32[256]{0:T(256)}, u32[]{:S(2)}) copy-start(s32[256]{0:T(256)} %param.14) | copy-start | bytes 3076
  163.9 21.4 %all-to-all-start.1 = ((bf16[16,16,2048]{2,0,1:T(8,128)(2,1)}), bf16[16,16,2048]{2,0,1:T(8,128)(2,1)S(1)}, u32[]{:S(2)}, u32[]{:S(2)}) async-start(bf16[16,16,2048]{2,0,1:T(8,128)(2,1)} %copy.49), calls=%async_computation.1 | async-start | bytes 2097152 | tf_op jit(solution)/shard_map/all_to_all | solution.py:31
  202.6 9.7 %copy-start.6 = (s32[256]{0:T(256)S(1)}, s32[256]{0:T(256)}, u32[]{:S(2)}) copy-start(s32[256]{0:T(256)} %param.13) | copy-start | bytes 3076
  445.5 22.6 %all-to-all-start.3 = ((bf16[16,16,2048]{2,0,1:T(8,128)(2,1)}), bf16[16,16,2048]{2,0,1:T(8,128)(2,1)S(1)}, u32[]{:S(2)}, u32[]{:S(2)}) async-start(bf16[16,16,2048]{2,0,1:T(8,128)(2,1)} %copy.64), calls=%async_computation.3 | async-start | bytes 2097152 | tf_op jit(solution)/shard_map/all_to_all | solution.py:31
  495.0 7.5 %copy-start.2 = (f32[16,128,64]{1,2,0:T(8,128)S(1)}, f32[16,128,64]{1,2,0:T(8,128)}, u32[]{:S(2)}) copy-start(f32[16,128,64]{1,2,0:T(8,128)} %get-tuple-element.11) | copy-start | bytes 1572868
  502.5 163.6 %copy-start.4 = (f32[192,64]{0,1:T(8,128)S(1)}, f32[192,64]{0,1:T(8,128)}, u32[]{:S(2)}) copy-start(f32[192,64]{0,1:T(8,128)} %param.18) | copy-start | bytes 147460
  502.5 165.5 %copy-start.1 = (f32[16,64,128]{2,1,0:T(8,128)S(1)}, f32[16,64,128]{2,1,0:T(8,128)}, u32[]{:S(2)}) copy-start(f32[16,64,128]{2,1,0:T(8,128)} %param.11) | copy-start | bytes 1572868
where the time goes:
time: 675 us; the launch traced here: 668 us
  blocking collectives  442 us (65%)
  local copies, waits for them, and re-layouts  93.1 us (14%)
  matrix products  45.1 us (7%)
  other arithmetic  44.5 us (7%)
  waiting for transfers between devices  35 us (5%)
  starting transfers between devices  7.75 us (1%)
    psum x2, blocking collectives, body(): lax.psum(local_inner(residual_block, residual_block), ('row', 'col'))  148 us
    psum x2, blocking collectives, body(): lax.psum(local_inner(stacked, product_block), ('row', 'col')) / node_total  146 us
    psum x1, blocking collectives, body(): start_sum = lax.psum(local_inner(start_block, start_block), ('row', 'col'))  81.5 us
    all_to_all x2, blocking collectives, apply_graph(): lax.all_to_all(outgoing, 'row', split_axis=0, concat_axis=0, tiled=True)  66.1 us
    gather x2, local copies, waits for them, and re-layouts, apply_graph(): node_rows[targets.reshape(-1)].reshape(partitions, capacity, block_width)  48.1 us
    all_to_all x2, waiting for transfers between devices, apply_graph(): lax.all_to_all(lax.all_to_all(outgoing, 'row', split_axis=0, concat_axis=...  35 us
    gather x2, local copies, waits for them, and re-layouts, apply_graph(): picked = source[tile_cols]  20.7 us
    another operation x9, other arithmetic, unit_columns(): factor = jnp.linalg.cholesky(gram_matrix)  19.6 us
  transfers between devices with their start and end apart: 2, of which 2 were waited for; matrix products, arithmetic and copies ran while one was open for 0% of the time, Pallas kernels for 0%

commit v1 on v0

--- a/solution.py
+++ b/solution.py
@@ -63,7 +63,9 @@
             vectors[-1], tile_values, tile_rows, tile_cols, tile_count, send_rows, send_count
         )
         stacked = jnp.concatenate(vectors, 1)
-        coefficients = lax.psum(local_inner(stacked, product_block), ("row", "col")) / node_total
+        coefficients = (
+            lax.psum(lax.psum(local_inner(stacked, product_block), "row"), "col") / node_total
+        )
         residual_block = product_block - jnp.einsum(
             "ab,tai->tbi", coefficients, stacked, precision=HIGHEST_PRECISION
         )

time: 675 us -> 756 us (1.12)
  blocking collectives: 442 us -> 523 us
    psum x2 -> x4, blocking collectives: 146 us -> 197 us  [the longest x2 112 us: body(): lax.psum(lax.psum(local_inner(stacked, product_block), 'row'), 'col')]
    psum x2, blocking collectives: 148 us -> 176 us  [body(): lax.psum(local_inner(residual_block, residual_block), ('row', 'col'))]
where the time goes in v1:
time: 756 us; the launch traced here: 750 us
  blocking collectives  523 us (69%)
  local copies, waits for them, and re-layouts  93.1 us (12%)
  matrix products  45.1 us (6%)
  other arithmetic  44.5 us (6%)
  waiting for transfers between devices  35 us (5%)
  starting transfers between devices  8.1 us (1%)
    psum x2, blocking collectives, body(): lax.psum(local_inner(residual_block, residual_block), ('row', 'col'))  176 us
    psum x2, blocking collectives, body(): lax.psum(lax.psum(local_inner(stacked, product_block), 'row'), 'col')  112 us
    psum x2, blocking collectives, body(): lax.psum(local_inner(stacked, product_block), 'row')  85.1 us
    psum x1, blocking collectives, body(): start_sum = lax.psum(local_inner(start_block, start_block), ('row', 'col'))  81.5 us
    all_to_all x2, blocking collectives, apply_graph(): lax.all_to_all(outgoing, 'row', split_axis=0, concat_axis=0, tiled=True)  67.4 us
    gather x2, local copies, waits for them, and re-layouts, apply_graph(): node_rows[targets.reshape(-1)].reshape(partitions, capacity, block_width)  48.1 us
    all_to_all x2, waiting for transfers between devices, apply_graph(): lax.all_to_all(lax.all_to_all(outgoing, 'row', split_axis=0, concat_axis=...  35 us
    gather x2, local copies, waits for them, and re-layouts, apply_graph(): picked = source[tile_cols]  20.7 us
  transfers between devices with their start and end apart: 2, of which 2 were waited for; matrix products, arithmetic and copies ran while one was open for 0% of the time, Pallas kernels for 0%

profile of v1, /device:TPU:1, one launch (start us, length us, event | category | flops | bytes accessed | tf_op | source)
XLA Modules:
  0.0 749.8 jit_solution(5239690706114066985)
XLA Ops:
  1.6 81.5 %psum.49 = f32[64,64]{0,1:T(8,128)S(1)} all-reduce(f32[64,64]{0,1:T(8,128)S(1)} %convolution_bitcast_fusion.8), channel_id=1, replica_groups=mesh['row'=16,'col'=16] {'row','col'}, use_global_device_ids=true, to_apply=%region_0.0 | all-reduce | flops 4096 | bytes 32768 | tf_op jit(solution)/shard_map/psum | solution.py:59
  83.2 5.8 cholesky.59
  90.4 4.9 custom-call.7
  96.8 24.0 %gather_fusion = bf16[8192,64]{1,0:T(8,128)(2,1)S(1)} fusion(bf16[2048,64]{1,0:T(8,128)(2,1)S(1)} %bitcast.92, s32[8192]{0:T(1024)S(1)} %broadcast_clamp_fusion), kind=kCustom, calls=%fused_computation | custom fusion | bytes 2129920 | tf_op jit(solution)/shard_map/gather | solution.py:27
  120.9 2.4 reshape.93
  128.8 33.5 %all_to_all.20 = bf16[16,16,2048]{2,1,0:T(8,128)(2,1)S(1)} all-to-all(bf16[16,16,2048]{2,1,0:T(8,128)(2,1)S(1)} %broadcast_select_fusion.1), channel_id=1, replica_groups=mesh['row'=16,'col'=16] {'row'}, dimensions={0} | all-to-all | bytes 2097152 | tf_op jit(solution)/shard_map/all_to_all | solution.py:32
  163.9 3.9 all-to-all-start.1
  168.7 16.5 %all-to-all-done.1 = bf16[16,16,2048]{2,0,1:T(8,128)(2,1)S(1)} async-done(((bf16[16,16,2048]{2,0,1:T(8,128)(2,1)}), bf16[16,16,2048]{2,0,1:T(8,128)(2,1)S(1)}, u32[]{:S(2)}, u32[]{:S(2)}) %all-to-all-start.1) | async-done | bytes 1048608 | tf_op jit(solution)/shard_map/all_to_all | solution.py:31
  186.8 3.3 reshape.94
  190.2 2.1 pad_maximum_fusion
  192.2 10.4 %gather_fusion.1 = bf16[256,64,128]{1,2,0:T(8,128)(2,1)} fusion(bf16[80,64,128]{1,2,0:T(8,128)(2,1)} %pad_maximum_fusion, s32[1024]{0:T(1024)S(1)} %pad_clamp_fusion), kind=kCustom, calls=%fused_computation.1 | custom fusion | bytes 8389632 | tf_op jit(solution)/shard_map/gather | solution.py:41
  202.6 9.7 %fusion.57 = f32[256,64,128]{2,1,0:T(8,128)S(1)} fusion(bf16[256,64,128]{1,2,0:T(8,128)(2,1)} %gather_fusion.1, bf16[256,128,128]{2,1,0:T(8,128)(2,1)} %param.12), kind=kOutput, calls=%fused_computation.100 | convolution fusion | flops 536870912 | bytes 20971520 | tf_op jit(solution)/shard_map/kbj,kij->kbi/dot_general | solution.py:42
  212.3 7.5 %fusion.2 = f32[16,64,128]{2,0,1:T(8,128)S(1)} fusion(f32[256,64,128]{2,1,0:T(8,128)S(1)} %fusion.57, s32[256]{0:T(256)S(1)} %copy-done.6, pred[256]{0:T(512)(128)(4,1)S(1)} %iota_compare_fusion.7), kind=kOutput, calls=%fused_computation.6 | convolution fusion | flops 402661376 | bytes 8914176 | tf_op jit(solution)/shard_map/rk,kbi->rbi/dot_general | solution.py:48
  220.5 42.5 %psum.50 = f32[64,64]{0,1:T(8,128)S(1)} all-reduce(f32[64,64]{0,1:T(8,128)S(1)} %convolution_bitcast_fusion.6), channel_id=1, replica_groups=mesh['row'=16,'col'=16] {'row'}, use_global_device_ids=true, to_apply=%region_3.0 | all-reduce | flops 4096 | bytes 32768 | tf_op jit(solution)/shard_map/psum | solution.py:67
  263.0 56.5 %psum.51 = f32[64,64]{0,1:T(8,128)S(1)} all-reduce(f32[64,64]{0,1:T(8,128)S(1)} %psum.50), channel_id=1, replica_groups=mesh['row'=16,'col'=16] {'col'}, use_global_device_ids=true, to_apply=%region_4.0 | all-reduce | flops 4096 | bytes 32768 | tf_op jit(solution)/shard_map/psum | solution.py:67
  321.3 88.0 %psum.52 = f32[64,64]{0,1:T(8,128)S(1)} all-reduce(f32[64,64]{0,1:T(8,128)S(1)} %convolution_bitcast_fusion.5), channel_id=1, replica_groups=mesh['row'=16,'col'=16] {'row','col'}, use_global_device_ids=true, to_apply=%region_5.0 | all-reduce | flops 4096 | bytes 32768 | tf_op jit(solution)/shard_map/psum | solution.py:73
  409.4 5.8 cholesky.70
  416.7 4.9 custom-call.8
  423.8 24.0 %gather_fusion.2 = bf16[8192,64]{1,0:T(8,128)(2,1)S(1)} fusion(bf16[2048,64]{1,0:T(8,128)(2,1)S(1)} %bitcast.93, s32[8192]{0:T(1024)S(1)} %broadcast_clamp_fusion), kind=kCustom, calls=%fused_computation.2 | custom fusion | bytes 2129920 | tf_op jit(solution)/shard_map/gather | solution.py:27
  447.8 2.4 reshape.96
  451.7 34.0 %all_to_all.21 = bf16[16,16,2048]{2,1,0:T(8,128)(2,1)S(1)} all-to-all(bf16[16,16,2048]{2,1,0:T(8,128)(2,1)S(1)} %broadcast_select_fusion), channel_id=1, replica_groups=mesh['row'=16,'col'=16] {'row'}, dimensions={0} | all-to-all | bytes 2097152 | tf_op jit(solution)/shard_map/all_to_all | solution.py:32
  487.3 4.2 all-to-all-start.3
  491.8 18.4 %all-to-all-done.3 = bf16[16,16,2048]{2,0,1:T(8,128)(2,1)S(1)} async-done(((bf16[16,16,2048]{2,0,1:T(8,128)(2,1)}), bf16[16,16,2048]{2,0,1:T(8,128)(2,1)S(1)}, u32[]{:S(2)}, u32[]{:S(2)}) %all-to-all-start.3) | async-done | bytes 1048608 | tf_op jit(solution)/shard_map/all_to_all | solution.py:31
  511.8 3.3 reshape.97
  517.2 10.4 %gather_fusion.3 = bf16[256,64,128]{1,2,0:T(8,128)(2,1)} fusion(bf16[80,64,128]{1,2,0:T(8,128)(2,1)} %pad_maximum_fusion.1, s32[1024]{0:T(1024)S(1)} %pad_clamp_fusion), kind=kCustom, calls=%fused_computation.3 | custom fusion | bytes 8389632 | tf_op jit(solution)/shard_map/gather | solution.py:41
  527.6 9.5 %fusion.58 = f32[256,64,128]{2,1,0:T(8,128)S(1)} fusion(bf16[256,64,128]{1,2,0:T(8,128)(2,1)} %gather_fusion.3, bf16[256,128,128]{2,1,0:T(8,128)(2,1)} %param.12), kind=kOutput, calls=%fused_computation.101 | convolution fusion | flops 536870912 | bytes 20971520 | tf_op jit(solution)/shard_map/kbj,kij->kbi/dot_general | solution.py:42
  537.1 7.5 %fusion = f32[16,64,128]{2,0,1:T(8,128)S(1)} fusion(f32[256,64,128]{2,1,0:T(8,128)S(1)} %fusion.58, s32[256]{0:T(256)S(1)} %copy-done.6, pred[256]{0:T(512)(128)(4,1)S(1)} %iota_compare_fusion.7), kind=kOutput, calls=%fused_computation.4 | convolution fusion | flops 402661376 | bytes 8914176 | tf_op jit(solution)/shard_map/rk,kbi->rbi/dot_general | solution.py:48
  545.8 42.5 %psum.53 = f32[128,64]{0,1:T(8,128)S(1)} all-reduce(f32[128,64]{0,1:T(8,128)S(1)} %convolution_bitcast_fusion.1), channel_id=1, replica_groups=mesh['row'=16,'col'=16] {'row'}, use_global_device_ids=true, to_apply=%region_6.0 | all-reduce | flops 8192 | bytes 65536 | tf_op jit(solution)/shard_map/psum | solution.py:67
  588.4 55.7 %psum.54 = f32[128,64]{0,1:T(8,128)S(1)} all-reduce(f32[128,64]{0,1:T(8,128)S(1)} %psum.53), channel_id=1, replica_groups=mesh['row'=16,'col'=16] {'col'}, use_global_device_ids=true, to_apply=%region_7.10 | all-reduce | flops 8192 | bytes 65536 | tf_op jit(solution)/shard_map/psum | solution.py:67
  645.9 88.3 %psum.55 = f32[64,64]{0,1:T(8,128)S(1)} all-reduce(f32[64,64]{0,1:T(8,128)S(1)} %convolution_bitcast_fusion.3), channel_id=1, replica_groups=mesh['row'=16,'col'=16] {'row','col'}, use_global_device_ids=true, to_apply=%region_8.11 | all-reduce | flops 4096 | bytes 32768 | tf_op jit(solution)/shard_map/psum | solution.py:73
  734.2 5.8 cholesky.81
  741.4 4.9 custom-call.9
  (74 shorter events, 33.8 us)
Async XLA Ops:
  0.0 1.0 copy-start
  0.0 96.5 %copy-start.5 = (s32[1,256,32]{1,2,0:T(8,128)S(1)}, s32[1,256,32]{1,2,0:T(8,128)}, u32[]{:S(2)}) copy-start(s32[1,256,32]{1,2,0:T(8,128)} %param.16) | copy-start | bytes 98308
  96.8 26.5 %copy-start.7 = (s32[1,256]{1,0:T(1,128)S(1)}, s32[1,256]{1,0:T(1,128)}, u32[]{:S(2)}) copy-start(s32[1,256]{1,0:T(1,128)} %param.17) | copy-start | bytes 3076
  127.3 36.6 %copy-start.3 = (pred[16,16,2048]{2,1,0:T(8,128)(4,1)}, pred[16,16,2048]{2,1,0:T(8,128)(4,1)S(1)}, u32[]{:S(2)}) copy-start(pred[16,16,2048]{2,1,0:T(8,128)(4,1)S(1)} %broadcast_in_dim.17) | copy-start | bytes 1572868
  128.8 39.9 %copy-start.8 = (s32[256]{0:T(256)S(1)}, s32[256]{0:T(256)}, u32[]{:S(2)}) copy-start(s32[256]{0:T(256)} %param.14) | copy-start | bytes 3076
  163.9 21.4 %all-to-all-start.1 = ((bf16[16,16,2048]{2,0,1:T(8,128)(2,1)}), bf16[16,16,2048]{2,0,1:T(8,128)(2,1)S(1)}, u32[]{:S(2)}, u32[]{:S(2)}) async-start(bf16[16,16,2048]{2,0,1:T(8,128)(2,1)} %copy.49), calls=%async_computation.1 | async-start | bytes 2097152 | tf_op jit(solution)/shard_map/all_to_all | solution.py:31
  202.6 9.7 %copy-start.6 = (s32[256]{0:T(256)S(1)}, s32[256]{0:T(256)}, u32[]{:S(2)}) copy-start(s32[256]{0:T(256)} %param.13) | copy-start | bytes 3076
  487.3 23.0 %all-to-all-start.3 = ((bf16[16,16,2048]{2,0,1:T(8,128)(2,1)}), bf16[16,16,2048]{2,0,1:T(8,128)(2,1)S(1)}, u32[]{:S(2)}, u32[]{:S(2)}) async-start(bf16[16,16,2048]{2,0,1:T(8,128)(2,1)} %copy.64), calls=%async_computation.3 | async-start | bytes 2097152 | tf_op jit(solution)/shard_map/all_to_all | solution.py:31
  537.1 7.5 %copy-start.2 = (f32[16,128,64]{1,2,0:T(8,128)S(1)}, f32[16,128,64]{1,2,0:T(8,128)}, u32[]{:S(2)}) copy-start(f32[16,128,64]{1,2,0:T(8,128)} %get-tuple-element.11) | copy-start | bytes 1572868
  544.6 202.7 %copy-start.4 = (f32[192,64]{0,1:T(8,128)S(1)}, f32[192,64]{0,1:T(8,128)}, u32[]{:S(2)}) copy-start(f32[192,64]{0,1:T(8,128)} %param.18) | copy-start | bytes 147460
  544.6 204.7 %copy-start.1 = (f32[16,64,128]{2,1,0:T(8,128)S(1)}, f32[16,64,128]{2,1,0:T(8,128)}, u32[]{:S(2)}) copy-start(f32[16,64,128]{2,1,0:T(8,128)} %param.11) | copy-start | bytes 1572868
